TPU v7x, 32 devices: a whole 2x2x4 slice. The times are simulated.
32 devices in a mesh: rep: 4 (over y, x), shard: 8 (over z, core).
Axes of the slice: x: 2, y: 2, z: 4, core: 2. Of those that a mesh axis runs over, the one named last changes fastest.
Arguments:
- tokens: bfloat16 [4096, 768], P(('rep', 'shard')), may hold values from -6 to 6
- segment_ids: int32 [32, 128], P(('rep', 'shard')), may hold values from 0 to 3, never falling along the last dimension, each value on 1 to 64 neighbouring positions
- first_gain: bfloat16 [768], P('shard'), may hold values from 0.5 to 1.5
- first_shift: bfloat16 [768], P('shard'), may hold values from -3 to 3
- qkv_weight: bfloat16 [768, 2304], P('shard'), may hold values from -3 to 3, as said below
- qv_bias: bfloat16 [2, 768], P(None, 'shard'), may hold values from -3 to 3
- proj_weight: bfloat16 [768, 768], P('shard'), may hold values from -0.625 to 0.625
- proj_bias: bfloat16 [768], P('shard'), may hold values from -3 to 3
- second_gain: bfloat16 [768], P('shard'), may hold values from 0.5 to 1.5
- second_shift: bfloat16 [768], P('shard'), may hold values from -3 to 3
- fc_weight: bfloat16 [768, 3072], P('shard'), may hold values from -0.21875 to 0.21875
- fc_bias: bfloat16 [3072], P('shard'), may hold values from -3 to 3
- out_weight: bfloat16 [3072, 768], P('shard'), may hold values from -0.109375 to 0.109375
- out_bias: bfloat16 [768], P('shard'), may hold values from -3 to 3
- cotangent: bfloat16 [4096, 768], P(('rep', 'shard')), may hold values from -6 to 6
Outputs:
- block_output: bfloat16 [4096, 768], P(('rep', 'shard'))
- grad_tokens: float32 [4096, 768], P(('rep', 'shard'))
- grad_first_gain: float32 [768], P('shard')
- grad_first_shift: float32 [768], P('shard')
- grad_qkv_weight: float32 [768, 2304], P('shard')
- grad_qv_bias: float32 [2, 768], P(None, 'shard')
- grad_proj_weight: float32 [768, 768], P('shard')
- grad_proj_bias: float32 [768], P('shard')
- grad_second_gain: float32 [768], P('shard')
- grad_second_shift: float32 [768], P('shard')
- grad_fc_weight: float32 [768, 3072], P('shard')
- grad_fc_bias: float32 [3072], P('shard')
- grad_out_weight: float32 [3072, 768], P('shard')
- grad_out_bias: float32 [768], P('shard')
Inputs may be any that keep to these rules, and one draw needn't show every extreme that they name: `segment_ids`: each row holds 4 runs of equal numbers in rising order, each run 1 to 64 long, one of them exactly 64. `qkv_weight`: columns 0 to 767 project to queries, the next 768 columns to keys, the last 768 columns to values.
All inputs are finite; a program needn't handle non-finite values.
Results may differ from a plain program's by a relative error of at most 0.011.
Values may be sent and summed in bfloat16 or wider, within the bound.
A program may use at most 128 MiB of HBM per device.

v0:
```python
import math
import jax
import jax.numpy as jnp
from jax import lax
from jax.sharding import PartitionSpec as P

D = 768
HEADS = 12
HD = 64
FF = 3072
EPSILON = 1e-05


def layer_norm(field, norm_gain, norm_shift):
    center = field - jnp.mean(field, axis=-1, keepdims=True)
    spread = jnp.mean(center * center, axis=-1, keepdims=True)
    return center * lax.rsqrt(spread + EPSILON) * norm_gain + norm_shift


def gelu_tanh(field):
    return jax.nn.gelu(field, approximate=True)


def head_split(matrix):
    return matrix.reshape(matrix.shape[0], HEADS, HD)


def masked_scores(query, keys, segments):
    rows = query.shape[0]
    scores = jnp.einsum(
        "qhd,khd->hqk", head_split(query), head_split(keys), preferred_element_type=jnp.float32
    ) * (1.0 / math.sqrt(HD))
    position = lax.iota(jnp.int32, rows)
    allowed = (segments[:, None] == segments[None, :]) & (position[None, :] <= position[:, None])
    return jnp.where(allowed[None], scores, -1e30)


def attend_forward(query, keys, values, segments):
    rows = query.shape[0]
    scores = masked_scores(query, keys, segments)
    row_max = jnp.max(scores, axis=-1, keepdims=True)
    row_total = jnp.sum(jnp.exp(scores - row_max), axis=-1, keepdims=True)
    logsum = row_max + jnp.log(row_total)
    probs = jnp.exp(scores - logsum).astype(jnp.bfloat16)
    attended = jnp.einsum(
        "hqk,khd->qhd", probs, head_split(values), preferred_element_type=jnp.float32
    )
    return (attended.reshape(rows, D).astype(jnp.bfloat16), logsum)


def attend_backward(query, keys, values, segments, attended, logsum, grad_attended):
    rows = query.shape[0]
    scores = masked_scores(query, keys, segments)
    weights = jnp.exp(scores - logsum)
    grad_heads = head_split(grad_attended)
    grad_values = jnp.einsum(
        "hqk,qhd->khd", weights.astype(jnp.bfloat16), grad_heads, preferred_element_type=jnp.float32
    )
    grad_probs = jnp.einsum(
        "qhd,khd->hqk", grad_heads, head_split(values), preferred_element_type=jnp.float32
    )
    delta = jnp.einsum(
        "qhd,qhd->hq", grad_heads, head_split(attended), preferred_element_type=jnp.float32
    )
    grad_scores = (weights * (grad_probs - delta[..., None]) * (1.0 / math.sqrt(HD))).astype(
        jnp.bfloat16
    )
    grad_query = jnp.einsum(
        "hqk,khd->qhd", grad_scores, head_split(keys), preferred_element_type=jnp.float32
    )
    grad_keys = jnp.einsum(
        "hqk,qhd->khd", grad_scores, head_split(query), preferred_element_type=jnp.float32
    )
    return (grad_query.reshape(rows, D), grad_keys.reshape(rows, D), grad_values.reshape(rows, D))


def exchange(field, axis, split, concat):
    return lax.all_to_all(field, axis, split_axis=split, concat_axis=concat, tiled=True)


def spread(field, axis):
    parts = lax.axis_size(axis)
    return exchange(jnp.broadcast_to(field[None], (parts,) + field.shape), axis, 0, 0)


def by_replica(field, shards, reps):
    rows = field.shape[0]
    return field.reshape(shards, reps, rows // (shards * reps), -1).swapaxes(0, 1).reshape(rows, -1)


def per_device(
    tokens,
    segment_ids,
    first_gain,
    first_shift,
    qkv_weight,
    qv_bias,
    proj_weight,
    proj_bias,
    second_gain,
    second_shift,
    fc_weight,
    fc_bias,
    out_weight,
    out_bias,
    cotangent,
):
    low = jnp.bfloat16
    segments = segment_ids[0]
    own_rows = tokens.shape[0]
    shards = lax.axis_size("shard")
    reps = lax.axis_size("rep")
    factor = 1.0 / math.sqrt(own_rows * reps * shards)
    small = jnp.stack(
        [
            first_gain,
            first_shift,
            qv_bias[0],
            qv_bias[1],
            proj_bias,
            second_gain,
            second_shift,
            out_bias,
        ]
    )
    small_full = lax.all_gather(small, "shard", axis=1, tiled=True).astype(jnp.float32)
    gain_one, shift_one, q_bias, v_bias, proj_bias_full, gain_two, shift_two, out_bias_full = (
        small_full[i] for i in range(8)
    )
    qkv_full = lax.all_gather(qkv_weight, "shard", axis=0, tiled=True)
    proj_full = lax.all_gather(proj_weight, "shard", axis=0, tiled=True)
    fc_cols = exchange(fc_weight, "shard", 1, 0)
    inputs = tokens.astype(jnp.float32)
    normed_f, first_back = jax.vjp(layer_norm, inputs, gain_one, shift_one)
    normed_first = normed_f.astype(low)
    projected = jnp.dot(normed_first, qkv_full, preferred_element_type=jnp.float32)
    query = (projected[:, :D] + q_bias).astype(low)
    keys = projected[:, D : 2 * D].astype(low)
    values = (projected[:, 2 * D :] + v_bias).astype(low)
    attended, logsum = attend_forward(query, keys, values, segments)
    residual = (
        inputs + jnp.dot(attended, proj_full, preferred_element_type=jnp.float32) + proj_bias_full
    )
    cot_f = cotangent.astype(jnp.float32)
    normed_s, second_back = jax.vjp(layer_norm, residual, gain_two, shift_two)
    normed_all = lax.all_gather(normed_s.astype(low), "shard", axis=0, tiled=True)
    cot_later, normed_all = lax.optimization_barrier((cotangent, normed_all))
    cot_all = lax.all_gather(cot_later, "shard", axis=0, tiled=True)
    pre_act = jnp.dot(normed_all, fc_cols, preferred_element_type=jnp.float32) + fc_bias.astype(
        jnp.float32
    )
    activated, gelu_back = jax.vjp(gelu_tanh, pre_act)
    hidden = activated.astype(low)
    grad_hidden = jnp.dot(cot_all, out_weight.T, preferred_element_type=jnp.float32)
    (grad_pre,) = gelu_back(grad_hidden)
    grad_pre_low = grad_pre.astype(low)
    grad_normed_part = jnp.dot(grad_pre_low, fc_cols.T, preferred_element_type=jnp.float32).astype(
        low
    )
    grad_normed_low = lax.psum_scatter(grad_normed_part, "shard", scatter_dimension=0, tiled=True)
    term_out_weight = jnp.dot(hidden.T, cot_all, preferred_element_type=jnp.float32) * factor
    term_fc_weight = (
        jnp.dot(normed_all.T, grad_pre_low, preferred_element_type=jnp.float32) * factor
    )
    out_part = jnp.dot(hidden, out_weight, preferred_element_type=jnp.float32).astype(low)
    ff_terms = jnp.concatenate(
        [
            term_out_weight.astype(low).reshape(reps, -1, D),
            by_replica(term_fc_weight.astype(low), shards, reps).reshape(reps, -1, D),
        ],
        axis=1,
    )
    ff_sum = jnp.sum(exchange(ff_terms, "rep", 0, 0).astype(jnp.float32), axis=0).astype(low)
    first_later, attended_later, grad_normed_low, ff_sum = lax.optimization_barrier(
        (normed_first, attended, grad_normed_low, ff_sum)
    )
    first_all = lax.all_gather(first_later, "shard", axis=0, tiled=True)
    grad_normed_second = grad_normed_low.astype(jnp.float32)
    grad_from_norm, second_gain_sum, second_shift_sum = second_back(grad_normed_second)
    grad_residual = cot_f + grad_from_norm
    grad_residual_low = grad_residual.astype(low)
    grad_residual_all = lax.all_gather(grad_residual_low, "shard", axis=0, tiled=True)
    attended_cols = exchange(attended_later, "shard", 1, 0)
    grad_attended = jnp.dot(
        grad_residual_low, proj_full.T, preferred_element_type=jnp.float32
    ).astype(low)
    out_rows = out_weight.shape[0] // reps
    out_piece = ff_sum[:out_rows]
    fc_piece = ff_sum[out_rows:].reshape(D // reps, -1)
    fc_piece = exchange(fc_piece, "shard", 0, 1)
    ff_all = spread(jnp.concatenate([out_piece, fc_piece.reshape(-1, D)]), "rep").astype(
        jnp.float32
    )
    grad_query, grad_keys, grad_values = attend_backward(
        query, keys, values, segments, attended, logsum, grad_attended
    )
    grad_projected = jnp.concatenate([grad_query, grad_keys, grad_values], axis=1).astype(low)
    grad_projected, ff_all = lax.optimization_barrier((grad_projected, ff_all))
    out_grad = ff_all[:, :out_rows].reshape(-1, D)
    fc_grad = ff_all[:, out_rows:].reshape(-1, FF)
    grad_cols = exchange(grad_projected, "shard", 1, 0)
    grad_normed_first = jnp.dot(grad_projected, qkv_full.T, preferred_element_type=jnp.float32)
    out_later, grad_cols = lax.optimization_barrier((out_part, grad_cols))
    out_sum = lax.psum_scatter(out_later, "shard", scatter_dimension=0, tiled=True)
    result = (residual + out_sum.astype(jnp.float32) + out_bias_full).astype(low)
    term_qkv_weight = jnp.dot(first_all.T, grad_cols, preferred_element_type=jnp.float32) * factor
    term_proj_weight = (
        jnp.dot(attended_cols.T, grad_residual_all, preferred_element_type=jnp.float32) * factor
    )
    attn_terms = jnp.concatenate(
        [
            term_proj_weight.astype(low).reshape(reps, -1, D),
            by_replica(term_qkv_weight.astype(low), shards, reps).reshape(reps, -1, D),
        ],
        axis=1,
    )
    attn_sum = jnp.sum(exchange(attn_terms, "rep", 0, 0).astype(jnp.float32), axis=0).astype(low)
    proj_rows = proj_weight.shape[0] // reps
    proj_piece = attn_sum[:proj_rows]
    qkv_piece = attn_sum[proj_rows:].reshape(D // reps, -1)
    qkv_piece = exchange(qkv_piece, "shard", 0, 1)
    attn_all = spread(jnp.concatenate([proj_piece, qkv_piece.reshape(-1, D)]), "rep").astype(
        jnp.float32
    )
    proj_grad = attn_all[:, :proj_rows].reshape(-1, D)
    qkv_grad = attn_all[:, proj_rows:].reshape(-1, 3 * D)
    grad_input_norm, first_gain_sum, first_shift_sum = first_back(grad_normed_first)
    grad_inputs = grad_residual + grad_input_norm
    terms = jnp.stack(
        [
            first_gain_sum,
            first_shift_sum,
            jnp.sum(grad_query, axis=0),
            jnp.sum(grad_values, axis=0),
            jnp.sum(grad_residual, axis=0),
            second_gain_sum,
            second_shift_sum,
            jnp.sum(cot_f, axis=0),
        ]
    )
    count = terms.shape[0]
    terms = terms.reshape(count, shards, -1).swapaxes(0, 1).reshape(shards, -1)
    own_terms = jnp.concatenate(
        [jnp.sum(exchange(terms, "shard", 0, 0), axis=0), jnp.sum(grad_pre, axis=0)]
    )
    sums = jnp.sum(spread(own_terms, "rep"), axis=0) * factor
    own_cols = D // shards
    fc_bias_grad = sums[count * own_cols :]
    sums = sums[: count * own_cols].reshape(count, own_cols)
    return (
        result,
        grad_inputs,
        sums[0],
        sums[1],
        qkv_grad,
        sums[2:4],
        proj_grad,
        sums[4],
        sums[5],
        sums[6],
        fc_grad,
        fc_bias_grad,
        out_grad,
        sums[7],
    )


def solution(mesh):
    return jax.shard_map(
        per_device,
        mesh=mesh,
        in_specs=(
            P(("rep", "shard"), None),
            P(("rep", "shard"), None),
            P("shard"),
            P("shard"),
            P("shard", None),
            P(None, "shard"),
            P("shard", None),
            P("shard"),
            P("shard"),
            P("shard"),
            P("shard", None),
            P("shard"),
            P("shard", None),
            P("shard"),
            P(("rep", "shard"), None),
        ),
        out_specs=(
            P(("rep", "shard"), None),
            P(("rep", "shard"), None),
            P("shard"),
            P("shard"),
            P("shard", None),
            P(None, "shard"),
            P("shard", None),
            P("shard"),
            P("shard"),
            P("shard"),
            P("shard", None),
            P("shard"),
            P("shard", None),
            P("shard"),
        ),
        check_vma=False,
    )
```

profile of v0, /device:TPU:0, one launch (start us, length us, event | category | flops | bytes accessed | tf_op | source)
XLA Modules:
  0.0 345.6 jit_solution(11735301634824392414)
XLA Ops:
  11.7 14.5 %all-gather = bf16[8,96,8]{1,2,0:T(8,128)(2,1)S(1)} all-gather(bf16[1,96,8]{1,2,0:T(8,128)(2,1)S(1)} %bitcast.133), channel_id=1, replica_groups=mesh['rep'=4,'shard'=8] {'shard'}, dimensions={0}, use_global_device_ids=true | all-gather | bytes 13824 | tf_op jit(solution)/shard_map/all_gather | solution.py:126
  28.9 25.1 %all-gather.8.cloned.1.call-done = bf16[768,2304]{1,0:T(8,128)(2,1)} async-done(((bf16[96,2304]{1,0:T(8,128)(2,1)}), bf16[768,2304]{1,0:T(8,128)(2,1)}) %all-gather.8.cloned.1.call-update) | async-done | bytes 3538960 | tf_op jit(solution)/shard_map/all_gather | solution.py:130
  53.9 2.6 fusion.57
  58.0 19.2 %all-gather.10.cloned.1.call-done = bf16[768,768]{1,0:T(8,128)(2,1)} async-done(((bf16[96,768]{1,0:T(8,128)(2,1)}), bf16[768,768]{1,0:T(8,128)(2,1)}) %all-gather.10.cloned.1.call-update) | async-done | bytes 1179664 | tf_op jit(solution)/shard_map/all_gather | solution.py:131
  77.2 1.8 fusion.56
  80.6 24.9 %all-gather.12.cloned.1.call-done = bf16[1024,768]{1,0:T(8,128)(2,1)} async-done(((bf16[128,768]{1,0:T(8,128)(2,1)}), bf16[1024,768]{1,0:T(8,128)(2,1)}) %all-gather.12.cloned.1.call-update) | async-done | bytes 1572880 | tf_op jit(solution)/shard_map/all_gather | solution.py:146
  106.4 3.5 %all-to-all-start = ((bf16[96,8,384]{2,0,1:T(8,128)(2,1)}), bf16[96,8,384]{2,0,1:T(8,128)(2,1)S(1)}, u32[]{:S(2)}, u32[]{:S(2)}) async-start(bf16[96,8,384]{2,0,1:T(8,128)(2,1)} %bitcast.106), calls=%async_computation | async-start | bytes 1179648 | tf_op jit(solution)/shard_map/all_to_all | solution.py:78
  110.0 30.8 %all-gather.14.cloned.1.call-done = bf16[1024,768]{1,0:T(8,128)(2,1)} async-done(((bf16[128,768]{1,0:T(8,128)(2,1)}), bf16[1024,768]{1,0:T(8,128)(2,1)}) %all-gather.14.cloned.1.call-update) | async-done | bytes 1572880 | tf_op jit(solution)/shard_map/all_gather | solution.py:148
  140.8 3.6 %fusion.58 = f32[1024,384]{1,0:T(8,128)} fusion(bf16[1024,768]{1,0:T(8,128)(2,1)} %all-gather.14.cloned.1.call-done, bf16[384,768]{1,0:T(8,128)(2,1)S(1)} %copy-done), kind=kOutput, calls=%fused_computation.119 | convolution fusion | flops 603979776 | bytes 3735552 | tf_op jit(solution)/shard_map/dot_general | solution.py:154
  144.4 5.6 %fusion.47 = (f32[384]{0:T(512)}, bf16[1024,384]{1,0:T(8,128)(2,1)S(1)}, f32[1024,384]{1,0:T(8,128)}) fusion(f32[1024,384]{1,0:T(8,128)} %fusion.58, f32[384]{0:T(512)S(1)} %convert_element_type.103, bf16[1024,768]{1,0:T(8,128)(2,1)} %all-gather.12.cloned.1.call-done, bf16[768,384]{1,0:T(8,128)(2,1)S(1)} %bitcast.125), kind=kOutput, calls=%fused_computation.109 | convolution fusion | flops 612630144 | bytes 6097920 | tf_op jit(solution)/shard_map/dot_general | solution.py:149
  150.9 2.2 convolution_convert_fusion
  153.1 2.6 fusion.7
  156.0 2.8 fusion.6
  158.9 19.4 %all_to_all.125 = bf16[4,192,768]{2,1,0:T(8,128)(2,1)S(1)} all-to-all(bf16[4,192,768]{2,1,0:T(8,128)(2,1)S(1)} %pad_maximum_fusion), channel_id=1, replica_groups=mesh['rep'=4,'shard'=8] {'rep'}, dimensions={0} | all-to-all | bytes 2359296 | tf_op jit(solution)/shard_map/all_to_all | solution.py:78
  179.2 7.8 %reduce-scatter.3.cloned.1.call-done = bf16[128,768]{1,0:T(8,128)(2,1)} async-done(((bf16[1024,768]{1,0:T(8,128)(2,1)}), bf16[128,768]{1,0:T(8,128)(2,1)}) %reduce-scatter.3.cloned.1.call-update) | async-done | bytes 196624 | tf_op jit(solution)/shard_map/reduce_scatter | solution.py:160
  187.1 1.7 fusion.53
  188.8 1.7 all_to_all.93
  190.5 4.0 %all-to-all-start.2 = ((bf16[8,24,384]{2,1,0:T(8,128)(2,1)}), bf16[8,24,384]{2,1,0:T(8,128)(2,1)}, u32[]{:S(2)}, u32[]{:S(2)}) async-start(bf16[8,24,384]{2,1,0:T(8,128)(2,1)} %all_to_all.93), calls=%async_computation.3 | async-start | bytes 294912 | tf_op jit(solution)/shard_map/all_to_all | solution.py:78
  194.6 1.8 fusion.30
  199.8 2.1 convolution_convert_fusion.3
  203.6 1.9 all-to-all-done.2
  207.6 4.6 %all-to-all-start.3 = ((bf16[4,192,768]{2,1,0:T(8,128)(2,1)}), bf16[4,192,768]{2,1,0:T(8,128)(2,1)}, u32[]{:S(2)}, u32[]{:S(2)}) async-start(bf16[4,192,768]{2,1,0:T(8,128)(2,1)} %broadcast_in_dim.34), calls=%async_computation.4 | async-start | bytes 2359296 | tf_op jit(solution)/shard_map/all_to_all | solution.py:78
  215.4 11.7 %all-to-all-done.3 = bf16[4,192,768]{2,1,0:T(8,128)(2,1)} async-done(((bf16[4,192,768]{2,1,0:T(8,128)(2,1)}), bf16[4,192,768]{2,1,0:T(8,128)(2,1)}, u32[]{:S(2)}, u32[]{:S(2)}) %all-to-all-start.3) | async-done | bytes 1179680 | tf_op jit(solution)/shard_map/all_to_all | solution.py:78
  227.1 1.5 convert_element_type.115
  228.6 4.2 %all-to-all-start.4 = ((bf16[128,8,288]{0,2,1:T(8,128)(2,1)}), bf16[128,8,288]{0,2,1:T(8,128)(2,1)}, u32[]{:S(2)}, u32[]{:S(2)}) async-start(bf16[128,8,288]{0,2,1:T(8,128)(2,1)} %bitcast.107), calls=%async_computation.5 | async-start | bytes 1179648 | tf_op jit(solution)/shard_map/all_to_all | solution.py:78
  232.8 3.8 %convolution_convert_fusion.1 = bf16[1024,768]{1,0:T(8,128)(2,1)} fusion(bf16[384,768]{1,0:T(8,128)(2,1)S(1)} %copy-done, f32[1024,384]{1,0:T(8,128)} %get-tuple-element.76), kind=kOutput, calls=%fused_computation.3 | convolution fusion | flops 608305152 | bytes 3735552 | tf_op jit(solution)/shard_map/dot_general | solution.py:165
  240.7 12.3 %all-to-all-done.4 = bf16[128,8,288]{0,2,1:T(8,128)(2,1)} async-done(((bf16[128,8,288]{0,2,1:T(8,128)(2,1)}), bf16[128,8,288]{0,2,1:T(8,128)(2,1)}, u32[]{:S(2)}, u32[]{:S(2)}) %all-to-all-start.4) | async-done | bytes 589856 | tf_op jit(solution)/shard_map/all_to_all | solution.py:78
  253.0 4.2 %all-to-all-start.7 = ((bf16[128,8,96]{0,2,1:T(8,128)(2,1)}), bf16[128,8,96]{0,2,1:T(8,128)(2,1)}, u32[]{:S(2)}, u32[]{:S(2)}) async-start(bf16[128,8,96]{0,2,1:T(8,128)(2,1)} %bitcast.109), calls=%async_computation.9 | async-start | bytes 393216 | tf_op jit(solution)/shard_map/all_to_all | solution.py:78
  257.2 2.0 copy_bitcast_fusion
  259.3 4.2 %fusion.46 = (f32[768]{0:T(1024)}, f32[128]{0:T(128)S(1)}, f32[128,768]{1,0:T(8,128)S(1)}) fusion(f32[768]{0:T(1024)S(1)} %get-tuple-element.50, f32[128]{0:T(128)S(1)} %copy-done.20, bf16[128,768]{1,0:T(8,128)(2,1)S(1)} %copy-done.1, bf16[128,2304]{0,1:T(8,128)(2,1)} %pad_maximum_fusion.1, bf16[768,2304]{1,0:T(8,128)(2,1)} %all-gather.8.cloned.1.call-done), kind=kOutput, calls=%fused_computation.108 | convolution fusion | flops 453573760 | bytes 4725760 | tf_op jit(solution)/shard_map/dot_general | solution.py:202
  267.3 3.0 fusion.11
  270.3 2.1 copy.150
  272.4 1.9 copy.151
  274.4 2.8 reshape_reshape.7
  277.1 5.0 %all-to-all-start.5 = ((f32[8,1,768]{2,1,0:T(1,128)}), f32[8,1,768]{2,1,0:T(1,128)S(1)}, u32[]{:S(2)}, u32[]{:S(2)}) async-start(f32[8,1,768]{2,1,0:T(1,128)} %all_to_all.113), calls=%async_computation.7 | async-start | bytes 49152 | tf_op jit(solution)/shard_map/all_to_all | solution.py:78
  282.1 2.0 fusion.14
  285.0 3.0 all-to-all-done.5
  288.0 4.2 %all-to-all-start.8 = ((bf16[4,96,768]{2,1,0:T(8,128)(2,1)}), bf16[4,96,768]{2,1,0:T(8,128)(2,1)}, u32[]{:S(2)}, u32[]{:S(2)}) async-start(bf16[4,96,768]{2,1,0:T(8,128)(2,1)} %pad_maximum_fusion.2), calls=%async_computation.10 | async-start | bytes 1179648 | tf_op jit(solution)/shard_map/all_to_all | solution.py:78
  292.3 9.2 %all-to-all-done.8 = bf16[4,96,768]{2,1,0:T(8,128)(2,1)} async-done(((bf16[4,96,768]{2,1,0:T(8,128)(2,1)}), bf16[4,96,768]{2,1,0:T(8,128)(2,1)}, u32[]{:S(2)}, u32[]{:S(2)}) %all-to-all-start.8) | async-done | bytes 589856 | tf_op jit(solution)/shard_map/all_to_all | solution.py:78
  302.1 3.3 all-to-all-start.6
  307.1 1.8 all_to_all.109
  310.0 4.0 %all-to-all-start.9 = ((bf16[8,24,288]{2,1,0:T(8,128)(2,1)}), bf16[8,24,288]{2,1,0:T(8,128)(2,1)}, u32[]{:S(2)}, u32[]{:S(2)}) async-start(bf16[8,24,288]{2,1,0:T(8,128)(2,1)} %all_to_all.109), calls=%async_computation.11 | async-start | bytes 294912 | tf_op jit(solution)/shard_map/all_to_all | solution.py:78
  314.0 1.7 fusion.50
  315.7 2.5 reshape.296
  318.3 2.8 all-to-all-done.9
  323.1 3.5 %all-to-all-start.10 = ((bf16[4,96,768]{2,1,0:T(8,128)(2,1)}), bf16[4,96,768]{2,1,0:T(8,128)(2,1)S(1)}, u32[]{:S(2)}, u32[]{:S(2)}) async-start(bf16[4,96,768]{2,1,0:T(8,128)(2,1)} %broadcast_in_dim.68), calls=%async_computation.12 | async-start | bytes 1179648 | tf_op jit(solution)/shard_map/all_to_all | solution.py:78
  328.5 6.6 %all-to-all-done.10 = bf16[4,96,768]{2,1,0:T(8,128)(2,1)S(1)} async-done(((bf16[4,96,768]{2,1,0:T(8,128)(2,1)}), bf16[4,96,768]{2,1,0:T(8,128)(2,1)S(1)}, u32[]{:S(2)}, u32[]{:S(2)}) %all-to-all-start.10) | async-done | bytes 589856 | tf_op jit(solution)/shard_map/all_to_all | solution.py:78
  337.1 1.7 add_convert_fusion
  (168 shorter events, 41.7 us)
Async XLA Ops:
  7.2 133.6 %copy-start = (bf16[384,768]{1,0:T(8,128)(2,1)S(1)}, bf16[384,768]{1,0:T(8,128)(2,1)}, u32[]{:S(2)}) copy-start(bf16[384,768]{1,0:T(8,128)(2,1)} %param.27) | copy-start | bytes 1769476
  7.2 46.7 %all-gather.8.cloned.1.call-start = ((), (), s32[]{:S(2)}) async-start(), calls=%async_computation.13 | async-start | bytes 3981312 | tf_op jit(solution)/shard_map/all_gather | solution.py:130
  7.9 69.2 %all-gather.10.cloned.1.call-start = ((), (), s32[]{:S(2)}) async-start(), calls=%async_computation.14 | async-start | bytes 1327104 | tf_op jit(solution)/shard_map/all_gather | solution.py:131
  8.7 96.8 %all-gather.12.cloned.1.call-start = ((), (), s32[]{:S(2)}) async-start(), calls=%async_computation.15 | async-start | bytes 1769472 | tf_op jit(solution)/shard_map/all_gather | solution.py:146
  9.8 46.8 %copy-start.19 = (f32[128]{0:T(128)}, f32[128]{0:T(128)S(1)}, u32[]{:S(2)}) copy-start(f32[128]{0:T(128)S(1)} %broadcast_multiply_fusion.2) | copy-start | bytes 1540
  10.9 45.7 %copy-start.23 = (f32[128]{0:T(128)}, f32[128]{0:T(128)S(1)}, u32[]{:S(2)}) copy-start(f32[128]{0:T(128)S(1)} %fusion.41) | copy-start | bytes 1540
  28.9 27.7 %copy-start.6 = (bf16[128,768]{1,0:T(8,128)(2,1)}, bf16[128,768]{1,0:T(8,128)(2,1)S(1)}, u32[]{:S(2)}) copy-start(bf16[128,768]{1,0:T(8,128)(2,1)S(1)} %fusion.25) | copy-start | bytes 589828
  56.9 1.1 copy-start.9
  57.1 0.9 copy-start.7
  57.2 19.9 %copy-start.1 = (bf16[128,768]{1,0:T(8,128)(2,1)S(1)}, bf16[128,768]{1,0:T(8,128)(2,1)}, u32[]{:S(2)}) copy-start(bf16[128,768]{1,0:T(8,128)(2,1)} %param.15) | copy-start | bytes 589828
  58.0 145.1 %copy-start.5 = (bf16[12,64,128]{2,1,0:T(8,128)(2,1)}, bf16[12,64,128]{2,1,0:T(8,128)(2,1)S(1)}, u32[]{:S(2)}) copy-start(bf16[12,64,128]{2,1,0:T(8,128)(2,1)S(1)} %convolution_convert_fusion.4) | copy-start | bytes 589828
  77.2 28.4 %copy-start.14 = (bf16[96,3072]{1,0:T(8,128)(2,1)S(1)}, bf16[96,3072]{1,0:T(8,128)(2,1)}, u32[]{:S(2)}) copy-start(bf16[96,3072]{1,0:T(8,128)(2,1)} %param.25) | copy-start | bytes 1769476
  78.9 27.5 %copy-start.22 = (f32[128]{0:T(128)}, f32[128]{0:T(128)S(1)}, u32[]{:S(2)}) copy-start(f32[128]{0:T(128)S(1)} %broadcast_multiply_fusion.1) | copy-start | bytes 1540
  79.2 27.2 %copy-start.25 = (f32[128]{0:T(128)}, f32[128]{0:T(128)S(1)}, u32[]{:S(2)}) copy-start(f32[128]{0:T(128)S(1)} %fusion.42) | copy-start | bytes 1540
  79.7 30.3 %copy-start.29 = (bf16[384]{0:T(512)(128)(2,1)S(1)}, bf16[384]{0:T(512)(128)(2,1)}, u32[]{:S(2)}) copy-start(bf16[384]{0:T(512)(128)(2,1)} %param.26) | copy-start | bytes 2308
  80.5 60.3 %all-gather.14.cloned.1.call-start = ((), (), s32[]{:S(2)}) async-start(), calls=%async_computation.16 | async-start | bytes 1769472 | tf_op jit(solution)/shard_map/all_gather | solution.py:148
  106.4 38.0 %all-to-all-start = ((bf16[96,8,384]{2,0,1:T(8,128)(2,1)}), bf16[96,8,384]{2,0,1:T(8,128)(2,1)S(1)}, u32[]{:S(2)}, u32[]{:S(2)}) async-start(bf16[96,8,384]{2,0,1:T(8,128)(2,1)} %bitcast.106), calls=%async_computation | async-start | bytes 1179648 | tf_op jit(solution)/shard_map/all_to_all | solution.py:78
  110.0 77.1 %reduce-scatter.3.cloned.1.call-start = ((), (), s32[]{:S(2)}) async-start(), calls=%async_computation.17 | async-start | bytes 1769472 | tf_op jit(solution)/shard_map/reduce_scatter | solution.py:160
  150.0 0.9 copy-start.33
  153.1 114.3 %all-gather.18.cloned.1.call-start = ((), (), s32[]{:S(2)}) async-start(), calls=%async_computation.20 | async-start | bytes 1769472 | tf_op jit(solution)/shard_map/all_gather | solution.py:177
  188.8 11.0 %copy-start.2 = (bf16[768,768]{1,0:T(8,128)(2,1)S(1)}, bf16[768,768]{1,0:T(8,128)(2,1)}, u32[]{:S(2)}) copy-start(bf16[768,768]{1,0:T(8,128)(2,1)} %all-gather.10.cloned.1.call-done) | copy-start | bytes 3538948
  190.5 14.9 %all-to-all-start.2 = ((bf16[8,24,384]{2,1,0:T(8,128)(2,1)}), bf16[8,24,384]{2,1,0:T(8,128)(2,1)}, u32[]{:S(2)}, u32[]{:S(2)}) async-start(bf16[8,24,384]{2,1,0:T(8,128)(2,1)} %all_to_all.93), calls=%async_computation.3 | async-start | bytes 294912 | tf_op jit(solution)/shard_map/all_to_all | solution.py:78
  194.5 87.6 %all-gather.16.cloned.1.call-start = ((), (), s32[]{:S(2)}) async-start(), calls=%async_computation.19 | async-start | bytes 1769472 | tf_op jit(solution)/shard_map/all_gather | solution.py:182
  194.6 4.4 %copy-start.12 = (bf16[128,768]{1,0:T(8,128)(2,1)S(1)}, bf16[128,768]{1,0:T(8,128)(2,1)}, u32[]{:S(2)}) copy-start(bf16[128,768]{1,0:T(8,128)(2,1)} %param.29) | copy-start | bytes 589828
  202.0 4.5 %copy-start.15 = (bf16[96,768]{1,0:T(8,128)(2,1)S(1)}, bf16[96,768]{1,0:T(8,128)(2,1)}, u32[]{:S(2)}) copy-start(bf16[96,768]{1,0:T(8,128)(2,1)} %get-tuple-element.64) | copy-start | bytes 442372
  206.5 5.7 %copy-start.10 = (bf16[128,768]{0,1:T(8,128)(2,1)S(1)}, bf16[128,768]{0,1:T(8,128)(2,1)}, u32[]{:S(2)}) copy-start(bf16[128,768]{0,1:T(8,128)(2,1)} %copy-done.9) | copy-start | bytes 589828
  207.6 5.0 %copy-start.8 = (bf16[128,768]{0,1:T(8,128)(2,1)S(1)}, bf16[128,768]{0,1:T(8,128)(2,1)}, u32[]{:S(2)}) copy-start(bf16[128,768]{0,1:T(8,128)(2,1)} %copy-done.7) | copy-start | bytes 589828
  207.6 19.6 %all-to-all-start.3 = ((bf16[4,192,768]{2,1,0:T(8,128)(2,1)}), bf16[4,192,768]{2,1,0:T(8,128)(2,1)}, u32[]{:S(2)}, u32[]{:S(2)}) async-start(bf16[4,192,768]{2,1,0:T(8,128)(2,1)} %broadcast_in_dim.34), calls=%async_computation.4 | async-start | bytes 2359296 | tf_op jit(solution)/shard_map/all_to_all | solution.py:78
  228.6 24.4 %all-to-all-start.4 = ((bf16[128,8,288]{0,2,1:T(8,128)(2,1)}), bf16[128,8,288]{0,2,1:T(8,128)(2,1)}, u32[]{:S(2)}, u32[]{:S(2)}) async-start(bf16[128,8,288]{0,2,1:T(8,128)(2,1)} %bitcast.107), calls=%async_computation.5 | async-start | bytes 1179648 | tf_op jit(solution)/shard_map/all_to_all | solution.py:78
  232.8 5.2 %copy-start.18 = (f32[768]{0:T(1024)S(1)}, f32[768]{0:T(1024)}, u32[]{:S(2)}) copy-start(f32[768]{0:T(1024)} %get-tuple-element.42) | copy-start | bytes 9220
  232.8 7.2 %copy-start.16 = (f32[12,64]{1,0:T(8,128)S(1)}, f32[12,64]{1,0:T(8,128)}, u32[]{:S(2)}) copy-start(f32[12,64]{1,0:T(8,128)} %get-tuple-element.62) | copy-start | bytes 9220
  253.0 6.2 %copy-start.20 = (f32[128]{0:T(128)S(1)}, f32[128]{0:T(128)}, u32[]{:S(2)}) copy-start(f32[128]{0:T(128)} %copy-done.19) | copy-start | bytes 1540
  253.0 24.1 %all-to-all-start.7 = ((bf16[128,8,96]{0,2,1:T(8,128)(2,1)}), bf16[128,8,96]{0,2,1:T(8,128)(2,1)}, u32[]{:S(2)}, u32[]{:S(2)}) async-start(bf16[128,8,96]{0,2,1:T(8,128)(2,1)} %bitcast.109), calls=%async_computation.9 | async-start | bytes 393216 | tf_op jit(solution)/shard_map/all_to_all | solution.py:78
  257.1 79.9 %reduce-scatter.5.cloned.1.call-start = ((), (), s32[]{:S(2)}) async-start(), calls=%async_computation.18 | async-start | bytes 1769472 | tf_op jit(solution)/shard_map/reduce_scatter | solution.py:204
  259.2 4.3 %copy-start.31 = (f32[128]{0:T(128)S(1)}, f32[128]{0:T(128)}, u32[]{:S(2)}) copy-start(f32[128]{0:T(128)} %copy-done.30) | copy-start | bytes 1540
  259.2 4.3 %copy-start.24 = (f32[128]{0:T(128)S(1)}, f32[128]{0:T(128)}, u32[]{:S(2)}) copy-start(f32[128]{0:T(128)} %copy-done.23) | copy-start | bytes 1540
  259.2 4.6 %copy-start.4 = (f32[128,768]{1,0:T(8,128)S(1)}, f32[128,768]{1,0:T(8,128)}, u32[]{:S(2)}) copy-start(f32[128,768]{1,0:T(8,128)} %copy-done.3) | copy-start | bytes 1179652
  259.2 4.6 %copy-start.13 = (bf16[128,768]{1,0:T(8,128)(2,1)S(1)}, bf16[128,768]{1,0:T(8,128)(2,1)}, u32[]{:S(2)}) copy-start(bf16[128,768]{1,0:T(8,128)(2,1)} %param.29) | copy-start | bytes 589828
  259.2 4.6 %copy-start.21 = (f32[128]{0:T(128)S(1)}, f32[128]{0:T(128)}, u32[]{:S(2)}) copy-start(f32[128]{0:T(128)} %copy-done.19) | copy-start | bytes 1540
  259.2 4.6 %copy-start.28 = (f32[128]{0:T(128)S(1)}, f32[128]{0:T(128)}, u32[]{:S(2)}) copy-start(f32[128]{0:T(128)} %copy-done.27) | copy-start | bytes 1540
  277.1 10.9 %all-to-all-start.5 = ((f32[8,1,768]{2,1,0:T(1,128)}), f32[8,1,768]{2,1,0:T(1,128)S(1)}, u32[]{:S(2)}, u32[]{:S(2)}) async-start(f32[8,1,768]{2,1,0:T(1,128)} %all_to_all.113), calls=%async_computation.7 | async-start | bytes 49152 | tf_op jit(solution)/shard_map/all_to_all | solution.py:78
  282.1 2.0 copy-start.11
  284.1 8.1 %copy-start.26 = (f32[384]{0:T(512)S(1)}, f32[384]{0:T(512)}, u32[]{:S(2)}) copy-start(f32[384]{0:T(512)} %get-tuple-element.51) | copy-start | bytes 4612
  288.0 13.4 %all-to-all-start.8 = ((bf16[4,96,768]{2,1,0:T(8,128)(2,1)}), bf16[4,96,768]{2,1,0:T(8,128)(2,1)}, u32[]{:S(2)}, u32[]{:S(2)}) async-start(bf16[4,96,768]{2,1,0:T(8,128)(2,1)} %pad_maximum_fusion.2), calls=%async_computation.10 | async-start | bytes 1179648 | tf_op jit(solution)/shard_map/all_to_all | solution.py:78
  302.1 7.9 %all-to-all-start.6 = ((f32[4,1,1152]{2,1,0:T(1,128)}), f32[4,1,1152]{2,1,0:T(1,128)S(1)}, u32[]{:S(2)}, u32[]{:S(2)}) async-start(f32[4,1,1152]{2,1,0:T(1,128)} %broadcast_in_dim.37), calls=%async_computation.8 | async-start | bytes 36864 | tf_op jit(solution)/shard_map/all_to_all | solution.py:78
  310.0 11.0 %all-to-all-start.9 = ((bf16[8,24,288]{2,1,0:T(8,128)(2,1)}), bf16[8,24,288]{2,1,0:T(8,128)(2,1)}, u32[]{:S(2)}, u32[]{:S(2)}) async-start(bf16[8,24,288]{2,1,0:T(8,128)(2,1)} %all_to_all.109), calls=%async_computation.11 | async-start | bytes 294912 | tf_op jit(solution)/shard_map/all_to_all | solution.py:78
  323.1 12.0 %all-to-all-start.10 = ((bf16[4,96,768]{2,1,0:T(8,128)(2,1)}), bf16[4,96,768]{2,1,0:T(8,128)(2,1)S(1)}, u32[]{:S(2)}, u32[]{:S(2)}) async-start(bf16[4,96,768]{2,1,0:T(8,128)(2,1)} %broadcast_in_dim.68), calls=%async_computation.12 | async-start | bytes 1179648 | tf_op jit(solution)/shard_map/all_to_all | solution.py:78
  335.2 1.9 copy-start.17
  (4 other events, 2.8 us)
Sparse Core Ops, SparseCore 0:
  9.7 44.2 all-gather.7
  55.6 21.5 all-gather.9
  80.6 24.8 all-gather.11
  107.0 33.7 all-gather.13
  153.2 33.8 reduce-scatter.2
  188.6 26.5 all-gather.17
  217.4 27.5 all-gather.15
  260.3 35.7 reduce-scatter.4
where the time goes:
time: 347 us; the launch traced here: 346 us
  waiting for transfers between devices  158 us (46%)
  starting transfers between devices  40.7 us (12%)
  local copies, waits for them, and re-layouts  40.4 us (12%)
  matrix products  39.6 us (11%)
  blocking collectives  33.9 us (10%)
  other arithmetic  18.2 us (5%)
  between operations  14.9 us (4%)
    all_to_all x10, waiting for transfers between devices, exchange(): lax.all_to_all(field, axis, split_axis=split, concat_axis=concat, tiled=T...  48.6 us
    all_to_all x10, starting transfers between devices, exchange(): lax.all_to_all(field, axis, split_axis=split, concat_axis=concat, tiled=T...  40.4 us
    all_gather x1, waiting for transfers between devices, per_device(): cot_all = lax.all_gather(cot_later, 'shard', axis=0, tiled=True)  30.8 us
    all_gather x1, waiting for transfers between devices, per_device(): qkv_full = lax.all_gather(qkv_weight, 'shard', axis=0, tiled=True)  25.1 us
    all_gather x1, waiting for transfers between devices, per_device(): lax.all_gather(normed_s.astype(low), 'shard', axis=0, tiled=True)  24.9 us
    all_to_all x1, blocking collectives, exchange(): lax.all_to_all(field, axis, split_axis=split, concat_axis=concat, tiled=T...  19.4 us
    all_gather x1, waiting for transfers between devices, per_device(): proj_full = lax.all_gather(proj_weight, 'shard', axis=0, tiled=True)  19.2 us
    all_gather x1, blocking collectives, per_device(): lax.all_gather(small, 'shard', axis=1, tiled=True).astype(jnp.float32)  14.5 us
  transfers between devices with their start and end apart: 18, of which 13 were waited for; matrix products, arithmetic and copies ran while one was open for 23% of the time, Pallas kernels for 0%

commit v1 on v0

--- a/solution.py
+++ b/solution.py
@@ -128,7 +128,14 @@
         small_full[i] for i in range(8)
     )
     qkv_full = lax.all_gather(qkv_weight, "shard", axis=0, tiled=True)
-    proj_full = lax.all_gather(proj_weight, "shard", axis=0, tiled=True)
+    ring = [proj_weight]
+    for hop in range(7):
+        ring.append(lax.ppermute(ring[-1], "shard", [(dev, (dev + 1) % 8) for dev in range(8)]))
+    proj_full = jnp.roll(
+        jnp.concatenate(ring[::-1], axis=0),
+        (lax.axis_index("shard") + 1) * ring[0].shape[0],
+        axis=0,
+    )
     fc_cols = exchange(fc_weight, "shard", 1, 0)
     inputs = tokens.astype(jnp.float32)
     normed_f, first_back = jax.vjp(layer_norm, inputs, gain_one, shift_one)

time: 347 us -> 354 us (1.020)
  local copies, waits for them, and re-layouts: 40.4 us -> 47.8 us
    ppermute x0 -> x7, waiting for transfers between devices: none -> 40.9 us  [per_device(): lax.ppermute(ring[-1], 'shard', [(dev, (dev + 1) % 8) for dev in range(8)])]
    all_gather x1, waiting for transfers between devices: 25.1 us -> 0.01 us  [per_device(): qkv_full = lax.all_gather(qkv_weight, 'shard', axis=0, tiled=True)]
    all_gather x1 -> x0, waiting for transfers between devices: 19.2 us -> none  [per_device(): proj_full = lax.all_gather(proj_weight, 'shard', axis=0, tiled=True)]
    unnamed x68 -> x91, local copies, waits for them, and re-layouts: 2.26 us -> 12.5 us
  transfers between devices with their start and end apart: 18 -> 24, of which waited for: 13 -> 17; matrix products, arithmetic and copies ran while one was open for 23% -> 23% of each run, Pallas kernels for 0% -> 0%
where the time goes in v1:
time: 354 us; the launch traced here: 352 us
  waiting for transfers between devices  156 us (44%)
  local copies, waits for them, and re-layouts  47.8 us (14%)
  starting transfers between devices  41.6 us (12%)
  matrix products  39.4 us (11%)
  blocking collectives  36.5 us (10%)
  other arithmetic  16 us (5%)
  between operations  14.9 us (4%)
    all_to_all x10, waiting for transfers between devices, exchange(): lax.all_to_all(field, axis, split_axis=split, concat_axis=concat, tiled=T...  52.1 us
    ppermute x7, waiting for transfers between devices, per_device(): lax.ppermute(ring[-1], 'shard', [(dev, (dev + 1) % 8) for dev in range(8)])  40.9 us
    all_to_all x10, starting transfers between devices, exchange(): lax.all_to_all(field, axis, split_axis=split, concat_axis=concat, tiled=T...  40.4 us
    all_gather x1, waiting for transfers between devices, per_device(): cot_all = lax.all_gather(cot_later, 'shard', axis=0, tiled=True)  30.8 us
    all_gather x1, waiting for transfers between devices, per_device(): lax.all_gather(normed_s.astype(low), 'shard', axis=0, tiled=True)  23.6 us
    all_to_all x1, blocking collectives, exchange(): lax.all_to_all(field, axis, split_axis=split, concat_axis=concat, tiled=T...  19.4 us
    all_gather x1, blocking collectives, per_device(): lax.all_gather(small, 'shard', axis=1, tiled=True).astype(jnp.float32)  17.1 us
    unnamed x91, local copies, waits for them, and re-layouts  12.5 us
  transfers between devices with their start and end apart: 24, of which 17 were waited for; matrix products, arithmetic and copies ran while one was open for 23% of the time, Pallas kernels for 0%

profile of v1, /device:TPU:0, one launch (start us, length us, event | category | flops | bytes accessed | tf_op | source)
XLA Modules:
  0.0 352.2 jit_solution(7122555303852812721)
XLA Ops:
  8.5 7.1 %collective-permute-done = bf16[96,768]{1,0:T(8,128)(2,1)S(1)} collective-permute-done((bf16[96,768]{1,0:T(8,128)(2,1)}, bf16[96,768]{1,0:T(8,128)(2,1)S(1)}, u32[]{:S(2)}, u32[]{:S(2)}) %collective-permute-start) | collective-permute-done | bytes 147488 | tf_op jit(solution)/shard_map/ppermute | solution.py:133
  15.6 6.4 %collective-permute-done.1 = bf16[96,768]{1,0:T(8,128)(2,1)S(1)} collective-permute-done((bf16[96,768]{1,0:T(8,128)(2,1)S(1)}, bf16[96,768]{1,0:T(8,128)(2,1)S(1)}, u32[]{:S(2)}, u32[]{:S(2)}) %collective-permute-start.1) | collective-permute-done | bytes 147488 | tf_op jit(solution)/shard_map/ppermute | solution.py:133
  23.0 8.5 %collective-permute-done.2 = bf16[96,768]{1,0:T(8,128)(2,1)S(1)} collective-permute-done((bf16[96,768]{1,0:T(8,128)(2,1)S(1)}, bf16[96,768]{1,0:T(8,128)(2,1)S(1)}, u32[]{:S(2)}, u32[]{:S(2)}) %collective-permute-start.2) | collective-permute-done | bytes 147488 | tf_op jit(solution)/shard_map/ppermute | solution.py:133
  32.6 8.4 %collective-permute-done.3 = bf16[96,768]{1,0:T(8,128)(2,1)S(1)} collective-permute-done((bf16[96,768]{1,0:T(8,128)(2,1)S(1)}, bf16[96,768]{1,0:T(8,128)(2,1)S(1)}, u32[]{:S(2)}, u32[]{:S(2)}) %collective-permute-start.3) | collective-permute-done | bytes 147488 | tf_op jit(solution)/shard_map/ppermute | solution.py:133
  41.8 17.1 %all-gather = bf16[8,96,8]{1,2,0:T(8,128)(2,1)S(1)} all-gather(bf16[1,96,8]{1,2,0:T(8,128)(2,1)S(1)} %bitcast.132), channel_id=1, replica_groups=mesh['rep'=4,'shard'=8] {'shard'}, dimensions={0}, use_global_device_ids=true | all-gather | bytes 13824 | tf_op jit(solution)/shard_map/all_gather | solution.py:126
  60.9 5.0 %collective-permute-done.5 = bf16[96,768]{1,0:T(8,128)(2,1)S(1)} collective-permute-done((bf16[96,768]{1,0:T(8,128)(2,1)S(1)}, bf16[96,768]{1,0:T(8,128)(2,1)S(1)}, u32[]{:S(2)}, u32[]{:S(2)}) %collective-permute-start.5) | collective-permute-done | bytes 147488 | tf_op jit(solution)/shard_map/ppermute | solution.py:133
  66.8 5.5 %collective-permute-done.6 = bf16[96,768]{1,0:T(8,128)(2,1)S(1)} collective-permute-done((bf16[96,768]{1,0:T(8,128)(2,1)S(1)}, bf16[96,768]{1,0:T(8,128)(2,1)S(1)}, u32[]{:S(2)}, u32[]{:S(2)}) %collective-permute-start.6) | collective-permute-done | bytes 147488 | tf_op jit(solution)/shard_map/ppermute | solution.py:133
  83.1 2.6 fusion.61
  87.3 1.9 fusion.60
  90.8 23.6 %all-gather.9.cloned.1.call-done = bf16[1024,768]{1,0:T(8,128)(2,1)} async-done(((bf16[128,768]{1,0:T(8,128)(2,1)}), bf16[1024,768]{1,0:T(8,128)(2,1)}) %all-gather.9.cloned.1.call-update) | async-done | bytes 1572880 | tf_op jit(solution)/shard_map/all_gather | solution.py:153
  115.3 3.5 %all-to-all-start = ((bf16[96,8,384]{2,0,1:T(8,128)(2,1)}), bf16[96,8,384]{2,0,1:T(8,128)(2,1)S(1)}, u32[]{:S(2)}, u32[]{:S(2)}) async-start(bf16[96,8,384]{2,0,1:T(8,128)(2,1)} %bitcast.104), calls=%async_computation | async-start | bytes 1179648 | tf_op jit(solution)/shard_map/all_to_all | solution.py:78
  119.0 30.8 %all-gather.11.cloned.1.call-done = bf16[1024,768]{1,0:T(8,128)(2,1)} async-done(((bf16[128,768]{1,0:T(8,128)(2,1)}), bf16[1024,768]{1,0:T(8,128)(2,1)}) %all-gather.11.cloned.1.call-update) | async-done | bytes 1572880 | tf_op jit(solution)/shard_map/all_gather | solution.py:155
  149.7 3.6 %fusion.62 = f32[1024,384]{1,0:T(8,128)} fusion(bf16[1024,768]{1,0:T(8,128)(2,1)} %all-gather.11.cloned.1.call-done, bf16[384,768]{1,0:T(8,128)(2,1)S(1)} %copy-done), kind=kOutput, calls=%fused_computation.139 | convolution fusion | flops 603979776 | bytes 3735552 | tf_op jit(solution)/shard_map/dot_general | solution.py:161
  153.3 5.5 %fusion.51 = (f32[384]{0:T(512)}, bf16[1024,384]{1,0:T(8,128)(2,1)S(1)}, f32[1024,384]{1,0:T(8,128)}) fusion(f32[1024,384]{1,0:T(8,128)} %fusion.62, f32[384]{0:T(512)S(1)} %convert_element_type.103, bf16[1024,768]{1,0:T(8,128)(2,1)} %all-gather.9.cloned.1.call-done, bf16[768,384]{1,0:T(8,128)(2,1)S(1)} %bitcast.123), kind=kOutput, calls=%fused_computation.129 | convolution fusion | flops 612630144 | bytes 6097920 | tf_op jit(solution)/shard_map/dot_general | solution.py:156
  159.7 2.2 convolution_convert_fusion
  161.9 2.6 fusion.7
  164.8 2.8 fusion.6
  167.7 19.4 %all_to_all.125 = bf16[4,192,768]{2,1,0:T(8,128)(2,1)S(1)} all-to-all(bf16[4,192,768]{2,1,0:T(8,128)(2,1)S(1)} %pad_maximum_fusion), channel_id=1, replica_groups=mesh['rep'=4,'shard'=8] {'rep'}, dimensions={0} | all-to-all | bytes 2359296 | tf_op jit(solution)/shard_map/all_to_all | solution.py:78
  188.1 7.8 %reduce-scatter.3.cloned.1.call-done = bf16[128,768]{1,0:T(8,128)(2,1)} async-done(((bf16[1024,768]{1,0:T(8,128)(2,1)}), bf16[128,768]{1,0:T(8,128)(2,1)}) %reduce-scatter.3.cloned.1.call-update) | async-done | bytes 196624 | tf_op jit(solution)/shard_map/reduce_scatter | solution.py:167
  197.7 3.4 all-to-all-start.2
  201.3 1.8 fusion.32
  204.2 1.9 convolution_convert_fusion.3
  206.8 3.5 all-to-all-done.2
  211.4 4.4 %all-to-all-start.3 = ((bf16[4,192,768]{2,1,0:T(8,128)(2,1)}), bf16[4,192,768]{2,1,0:T(8,128)(2,1)}, u32[]{:S(2)}, u32[]{:S(2)}) async-start(bf16[4,192,768]{2,1,0:T(8,128)(2,1)} %broadcast_in_dim.34), calls=%async_computation.4 | async-start | bytes 2359296 | tf_op jit(solution)/shard_map/all_to_all | solution.py:78
  219.1 10.9 %all-to-all-done.3 = bf16[4,192,768]{2,1,0:T(8,128)(2,1)} async-done(((bf16[4,192,768]{2,1,0:T(8,128)(2,1)}), bf16[4,192,768]{2,1,0:T(8,128)(2,1)}, u32[]{:S(2)}, u32[]{:S(2)}) %all-to-all-start.3) | async-done | bytes 1179680 | tf_op jit(solution)/shard_map/all_to_all | solution.py:78
  231.6 5.1 %all-to-all-start.4 = ((bf16[128,8,288]{0,2,1:T(8,128)(2,1)}), bf16[128,8,288]{0,2,1:T(8,128)(2,1)}, u32[]{:S(2)}, u32[]{:S(2)}) async-start(bf16[128,8,288]{0,2,1:T(8,128)(2,1)} %bitcast.105), calls=%async_computation.5 | async-start | bytes 1179648 | tf_op jit(solution)/shard_map/all_to_all | solution.py:78
  236.7 3.8 %convolution_convert_fusion.1 = bf16[1024,768]{1,0:T(8,128)(2,1)} fusion(bf16[384,768]{1,0:T(8,128)(2,1)S(1)} %copy-done, f32[1024,384]{1,0:T(8,128)} %get-tuple-element.76), kind=kOutput, calls=%fused_computation.3 | convolution fusion | flops 608305152 | bytes 3735552 | tf_op jit(solution)/shard_map/dot_general | solution.py:172
  244.6 15.0 %all-to-all-done.4 = bf16[128,8,288]{0,2,1:T(8,128)(2,1)} async-done(((bf16[128,8,288]{0,2,1:T(8,128)(2,1)}), bf16[128,8,288]{0,2,1:T(8,128)(2,1)}, u32[]{:S(2)}, u32[]{:S(2)}) %all-to-all-start.4) | async-done | bytes 589856 | tf_op jit(solution)/shard_map/all_to_all | solution.py:78
  259.6 4.1 %all-to-all-start.7 = ((bf16[128,8,96]{0,2,1:T(8,128)(2,1)}), bf16[128,8,96]{0,2,1:T(8,128)(2,1)}, u32[]{:S(2)}, u32[]{:S(2)}) async-start(bf16[128,8,96]{0,2,1:T(8,128)(2,1)} %bitcast.107), calls=%async_computation.9 | async-start | bytes 393216 | tf_op jit(solution)/shard_map/all_to_all | solution.py:78
  263.8 2.0 copy_bitcast_fusion
  265.9 4.2 %fusion.50 = (f32[768]{0:T(1024)}, f32[128]{0:T(128)S(1)}, f32[128,768]{1,0:T(8,128)S(1)}) fusion(f32[768]{0:T(1024)S(1)} %get-tuple-element.50, f32[128]{0:T(128)S(1)} %copy-done.21, bf16[128,768]{1,0:T(8,128)(2,1)S(1)} %copy-done.1, bf16[128,2304]{0,1:T(8,128)(2,1)} %pad_maximum_fusion.1, bf16[768,2304]{1,0:T(8,128)(2,1)} %all-gather.7.cloned.1.call-done), kind=kOutput, calls=%fused_computation.128 | convolution fusion | flops 453573760 | bytes 4725760 | tf_op jit(solution)/shard_map/dot_general | solution.py:209
  273.9 3.0 fusion.11
  277.0 2.1 copy.150
  279.0 1.9 copy.151
  281.0 2.8 reshape_reshape.7
  283.7 5.0 %all-to-all-start.5 = ((f32[8,1,768]{2,1,0:T(1,128)}), f32[8,1,768]{2,1,0:T(1,128)S(1)}, u32[]{:S(2)}, u32[]{:S(2)}) async-start(f32[8,1,768]{2,1,0:T(1,128)} %all_to_all.113), calls=%async_computation.7 | async-start | bytes 49152 | tf_op jit(solution)/shard_map/all_to_all | solution.py:78
  288.7 2.0 fusion.14
  291.6 3.0 all-to-all-done.5
  294.6 4.2 %all-to-all-start.8 = ((bf16[4,96,768]{2,1,0:T(8,128)(2,1)}), bf16[4,96,768]{2,1,0:T(8,128)(2,1)}, u32[]{:S(2)}, u32[]{:S(2)}) async-start(bf16[4,96,768]{2,1,0:T(8,128)(2,1)} %pad_maximum_fusion.2), calls=%async_computation.10 | async-start | bytes 1179648 | tf_op jit(solution)/shard_map/all_to_all | solution.py:78
  298.9 9.2 %all-to-all-done.8 = bf16[4,96,768]{2,1,0:T(8,128)(2,1)} async-done(((bf16[4,96,768]{2,1,0:T(8,128)(2,1)}), bf16[4,96,768]{2,1,0:T(8,128)(2,1)}, u32[]{:S(2)}, u32[]{:S(2)}) %all-to-all-start.8) | async-done | bytes 589856 | tf_op jit(solution)/shard_map/all_to_all | solution.py:78
  308.7 3.3 all-to-all-start.6
  313.7 1.8 all_to_all.109
  316.6 4.0 %all-to-all-start.9 = ((bf16[8,24,288]{2,1,0:T(8,128)(2,1)}), bf16[8,24,288]{2,1,0:T(8,128)(2,1)}, u32[]{:S(2)}, u32[]{:S(2)}) async-start(bf16[8,24,288]{2,1,0:T(8,128)(2,1)} %all_to_all.109), calls=%async_computation.11 | async-start | bytes 294912 | tf_op jit(solution)/shard_map/all_to_all | solution.py:78
  322.3 2.5 reshape.296
  324.8 2.8 all-to-all-done.9
  329.7 3.5 all-to-all-start.10
  335.1 6.6 %all-to-all-done.10 = bf16[4,96,768]{2,1,0:T(8,128)(2,1)S(1)} async-done(((bf16[4,96,768]{2,1,0:T(8,128)(2,1)}), bf16[4,96,768]{2,1,0:T(8,128)(2,1)S(1)}, u32[]{:S(2)}, u32[]{:S(2)}) %all-to-all-start.10) | async-done | bytes 589856 | tf_op jit(solution)/shard_map/all_to_all | solution.py:78
  343.7 1.7 add_convert_fusion
  (203 shorter events, 53.6 us)
Async XLA Ops:
  7.2 142.6 %copy-start = (bf16[384,768]{1,0:T(8,128)(2,1)S(1)}, bf16[384,768]{1,0:T(8,128)(2,1)}, u32[]{:S(2)}) copy-start(bf16[384,768]{1,0:T(8,128)(2,1)} %param.27) | copy-start | bytes 1769476
  7.2 75.9 %all-gather.7.cloned.1.call-start = ((), (), s32[]{:S(2)}) async-start(), calls=%async_computation.13 | async-start | bytes 3981312 | tf_op jit(solution)/shard_map/all_gather | solution.py:130
  7.9 69.1 %copy-start.16 = (bf16[96,768]{1,0:T(8,128)(2,1)S(1)}, bf16[96,768]{1,0:T(8,128)(2,1)}, u32[]{:S(2)}) copy-start(bf16[96,768]{1,0:T(8,128)(2,1)} %param.21) | copy-start | bytes 442372
  7.9 106.5 %all-gather.9.cloned.1.call-start = ((), (), s32[]{:S(2)}) async-start(), calls=%async_computation.14 | async-start | bytes 1769472 | tf_op jit(solution)/shard_map/all_gather | solution.py:153
  8.0 7.6 %collective-permute-start = (bf16[96,768]{1,0:T(8,128)(2,1)}, bf16[96,768]{1,0:T(8,128)(2,1)S(1)}, u32[]{:S(2)}, u32[]{:S(2)}) collective-permute-start(bf16[96,768]{1,0:T(8,128)(2,1)} %param.21), channel_id=1, source_target_pairs={{0,1},{1,2},{2,3},{3,4},{4,5},{5,6},{6,7},{7,0},{8,9},{9,10},{10,1... | collective-permute-start | bytes 442376 | tf_op jit(solution)/shard_map/ppermute | solution.py:133
  15.6 6.4 %collective-permute-start.1 = (bf16[96,768]{1,0:T(8,128)(2,1)S(1)}, bf16[96,768]{1,0:T(8,128)(2,1)S(1)}, u32[]{:S(2)}, u32[]{:S(2)}) collective-permute-start(bf16[96,768]{1,0:T(8,128)(2,1)S(1)} %collective-permute-done), channel_id=1, source_target_pairs={{0,1},{1,2},{2,3},{3,4},{4,5},{5,6},{6,7},{7,0},{8,9},{9,10},{10,1... | collective-permute-start | bytes 442376 | tf_op jit(solution)/shard_map/ppermute | solution.py:133
  21.9 9.5 %collective-permute-start.2 = (bf16[96,768]{1,0:T(8,128)(2,1)S(1)}, bf16[96,768]{1,0:T(8,128)(2,1)S(1)}, u32[]{:S(2)}, u32[]{:S(2)}) collective-permute-start(bf16[96,768]{1,0:T(8,128)(2,1)S(1)} %collective-permute-done.1), channel_id=1, source_target_pairs={{0,1},{1,2},{2,3},{3,4},{4,5},{5,6},{6,7},{7,0},{8,9},{9,10},{10,1... | collective-permute-start | bytes 442376 | tf_op jit(solution)/shard_map/ppermute | solution.py:133
  31.4 9.5 %collective-permute-start.3 = (bf16[96,768]{1,0:T(8,128)(2,1)S(1)}, bf16[96,768]{1,0:T(8,128)(2,1)S(1)}, u32[]{:S(2)}, u32[]{:S(2)}) collective-permute-start(bf16[96,768]{1,0:T(8,128)(2,1)S(1)} %collective-permute-done.2), channel_id=1, source_target_pairs={{0,1},{1,2},{2,3},{3,4},{4,5},{5,6},{6,7},{7,0},{8,9},{9,10},{10,1... | collective-permute-start | bytes 442376 | tf_op jit(solution)/shard_map/ppermute | solution.py:133
  31.4 46.2 %copy-start.20 = (f32[128]{0:T(128)}, f32[128]{0:T(128)S(1)}, u32[]{:S(2)}) copy-start(f32[128]{0:T(128)S(1)} %broadcast_multiply_fusion.2) | copy-start | bytes 1540
  32.6 8.5 %copy-start.33 = (f32[128]{0:T(128)}, f32[128]{0:T(128)S(1)}, u32[]{:S(2)}) copy-start(f32[128]{0:T(128)S(1)} %fusion.30) | copy-start | bytes 1540
  41.0 18.6 %collective-permute-start.4 = (bf16[96,768]{1,0:T(8,128)(2,1)S(1)}, bf16[96,768]{1,0:T(8,128)(2,1)S(1)}, u32[]{:S(2)}, u32[]{:S(2)}) collective-permute-start(bf16[96,768]{1,0:T(8,128)(2,1)S(1)} %collective-permute-done.3), channel_id=1, source_target_pairs={{0,1},{1,2},{2,3},{3,4},{4,5},{5,6},{6,7},{7,0},{8,9},{9,10},{10,1... | collective-permute-start | bytes 442376 | tf_op jit(solution)/shard_map/ppermute | solution.py:133
  41.0 37.4 %copy-start.25 = (f32[128]{0:T(128)}, f32[128]{0:T(128)S(1)}, u32[]{:S(2)}) copy-start(f32[128]{0:T(128)S(1)} %fusion.45) | copy-start | bytes 1540
  59.6 6.4 %collective-permute-start.5 = (bf16[96,768]{1,0:T(8,128)(2,1)S(1)}, bf16[96,768]{1,0:T(8,128)(2,1)S(1)}, u32[]{:S(2)}, u32[]{:S(2)}) collective-permute-start(bf16[96,768]{1,0:T(8,128)(2,1)S(1)} %collective-permute-done.4), channel_id=1, source_target_pairs={{0,1},{1,2},{2,3},{3,4},{4,5},{5,6},{6,7},{7,0},{8,9},{9,10},{10,1... | collective-permute-start | bytes 442376 | tf_op jit(solution)/shard_map/ppermute | solution.py:133
  60.9 22.2 %copy-start.5 = (bf16[128,768]{1,0:T(8,128)(2,1)}, bf16[128,768]{1,0:T(8,128)(2,1)S(1)}, u32[]{:S(2)}) copy-start(bf16[128,768]{1,0:T(8,128)(2,1)S(1)} %fusion.27) | copy-start | bytes 589828
  66.0 6.4 %collective-permute-start.6 = (bf16[96,768]{1,0:T(8,128)(2,1)S(1)}, bf16[96,768]{1,0:T(8,128)(2,1)S(1)}, u32[]{:S(2)}, u32[]{:S(2)}) collective-permute-start(bf16[96,768]{1,0:T(8,128)(2,1)S(1)} %collective-permute-done.5), channel_id=1, source_target_pairs={{0,1},{1,2},{2,3},{3,4},{4,5},{5,6},{6,7},{7,0},{8,9},{9,10},{10,1... | collective-permute-start | bytes 442376 | tf_op jit(solution)/shard_map/ppermute | solution.py:133
  87.1 119.2 %copy-start.4 = (bf16[12,64,128]{2,1,0:T(8,128)(2,1)}, bf16[12,64,128]{2,1,0:T(8,128)(2,1)S(1)}, u32[]{:S(2)}) copy-start(bf16[12,64,128]{2,1,0:T(8,128)(2,1)S(1)} %convolution_convert_fusion.4) | copy-start | bytes 589828
  87.3 27.2 %copy-start.15 = (bf16[96,3072]{1,0:T(8,128)(2,1)S(1)}, bf16[96,3072]{1,0:T(8,128)(2,1)}, u32[]{:S(2)}) copy-start(bf16[96,3072]{1,0:T(8,128)(2,1)} %param.25) | copy-start | bytes 1769476
  89.2 26.1 %copy-start.23 = (f32[128]{0:T(128)}, f32[128]{0:T(128)S(1)}, u32[]{:S(2)}) copy-start(f32[128]{0:T(128)S(1)} %broadcast_multiply_fusion.1) | copy-start | bytes 1540
  89.4 25.9 %copy-start.27 = (f32[128]{0:T(128)}, f32[128]{0:T(128)S(1)}, u32[]{:S(2)}) copy-start(f32[128]{0:T(128)S(1)} %fusion.46) | copy-start | bytes 1540
  89.9 29.0 %copy-start.32 = (bf16[384]{0:T(512)(128)(2,1)S(1)}, bf16[384]{0:T(512)(128)(2,1)}, u32[]{:S(2)}) copy-start(bf16[384]{0:T(512)(128)(2,1)} %param.26) | copy-start | bytes 2308
  90.7 59.0 %all-gather.11.cloned.1.call-start = ((), (), s32[]{:S(2)}) async-start(), calls=%async_computation.15 | async-start | bytes 1769472 | tf_op jit(solution)/shard_map/all_gather | solution.py:155
  115.3 38.0 %all-to-all-start = ((bf16[96,8,384]{2,0,1:T(8,128)(2,1)}), bf16[96,8,384]{2,0,1:T(8,128)(2,1)S(1)}, u32[]{:S(2)}, u32[]{:S(2)}) async-start(bf16[96,8,384]{2,0,1:T(8,128)(2,1)} %bitcast.104), calls=%async_computation | async-start | bytes 1179648 | tf_op jit(solution)/shard_map/all_to_all | solution.py:78
  118.9 77.0 %reduce-scatter.3.cloned.1.call-start = ((), (), s32[]{:S(2)}) async-start(), calls=%async_computation.16 | async-start | bytes 1769472 | tf_op jit(solution)/shard_map/reduce_scatter | solution.py:167
  161.9 112.1 %all-gather.15.cloned.1.call-start = ((), (), s32[]{:S(2)}) async-start(), calls=%async_computation.19 | async-start | bytes 1769472 | tf_op jit(solution)/shard_map/all_gather | solution.py:184
  188.1 15.0 %copy-start.36 = (f32[128]{0:T(128)S(1)}, f32[128]{0:T(128)}, u32[]{:S(2)}) copy-start(f32[128]{0:T(128)} %copy-done.35) | copy-start | bytes 1540
  188.1 15.0 %copy-start.24 = (f32[128]{0:T(128)S(1)}, f32[128]{0:T(128)}, u32[]{:S(2)}) copy-start(f32[128]{0:T(128)} %copy-done.23) | copy-start | bytes 1540
  188.1 15.0 %copy-start.28 = (f32[128]{0:T(128)S(1)}, f32[128]{0:T(128)}, u32[]{:S(2)}) copy-start(f32[128]{0:T(128)} %copy-done.27) | copy-start | bytes 1540
  188.1 16.0 %copy-start.11 = (bf16[128,768]{1,0:T(8,128)(2,1)S(1)}, bf16[128,768]{1,0:T(8,128)(2,1)}, u32[]{:S(2)}) copy-start(bf16[128,768]{1,0:T(8,128)(2,1)} %param.29) | copy-start | bytes 589828
  195.9 7.2 %copy-start.14 = (bf16[128,768]{1,0:T(8,128)(2,1)S(1)}, bf16[128,768]{1,0:T(8,128)(2,1)}, u32[]{:S(2)}) copy-start(bf16[128,768]{1,0:T(8,128)(2,1)} %reduce-scatter.3.cloned.1.call-done) | copy-start | bytes 589828
  197.7 12.6 %all-to-all-start.2 = ((bf16[8,24,384]{2,1,0:T(8,128)(2,1)}), bf16[8,24,384]{2,1,0:T(8,128)(2,1)S(1)}, u32[]{:S(2)}, u32[]{:S(2)}) async-start(bf16[8,24,384]{2,1,0:T(8,128)(2,1)} %all_to_all.93), calls=%async_computation.3 | async-start | bytes 294912 | tf_op jit(solution)/shard_map/all_to_all | solution.py:78
  201.0 87.7 %all-gather.13.cloned.1.call-start = ((), (), s32[]{:S(2)}) async-start(), calls=%async_computation.18 | async-start | bytes 1769472 | tf_op jit(solution)/shard_map/all_gather | solution.py:189
  210.3 5.5 %copy-start.9 = (bf16[128,768]{0,1:T(8,128)(2,1)S(1)}, bf16[128,768]{0,1:T(8,128)(2,1)}, u32[]{:S(2)}) copy-start(bf16[128,768]{0,1:T(8,128)(2,1)} %copy-done.8) | copy-start | bytes 589828
  211.4 4.8 %copy-start.7 = (bf16[128,768]{0,1:T(8,128)(2,1)S(1)}, bf16[128,768]{0,1:T(8,128)(2,1)}, u32[]{:S(2)}) copy-start(bf16[128,768]{0,1:T(8,128)(2,1)} %copy-done.6) | copy-start | bytes 589828
  211.4 18.6 %all-to-all-start.3 = ((bf16[4,192,768]{2,1,0:T(8,128)(2,1)}), bf16[4,192,768]{2,1,0:T(8,128)(2,1)}, u32[]{:S(2)}, u32[]{:S(2)}) async-start(bf16[4,192,768]{2,1,0:T(8,128)(2,1)} %broadcast_in_dim.34), calls=%async_computation.4 | async-start | bytes 2359296 | tf_op jit(solution)/shard_map/all_to_all | solution.py:78
  231.6 28.0 %all-to-all-start.4 = ((bf16[128,8,288]{0,2,1:T(8,128)(2,1)}), bf16[128,8,288]{0,2,1:T(8,128)(2,1)}, u32[]{:S(2)}, u32[]{:S(2)}) async-start(bf16[128,8,288]{0,2,1:T(8,128)(2,1)} %bitcast.105), calls=%async_computation.5 | async-start | bytes 1179648 | tf_op jit(solution)/shard_map/all_to_all | solution.py:78
  236.7 5.2 %copy-start.19 = (f32[768]{0:T(1024)S(1)}, f32[768]{0:T(1024)}, u32[]{:S(2)}) copy-start(f32[768]{0:T(1024)} %get-tuple-element.42) | copy-start | bytes 9220
  236.7 7.2 %copy-start.17 = (f32[12,64]{1,0:T(8,128)S(1)}, f32[12,64]{1,0:T(8,128)}, u32[]{:S(2)}) copy-start(f32[12,64]{1,0:T(8,128)} %get-tuple-element.62) | copy-start | bytes 9220
  259.6 6.2 %copy-start.21 = (f32[128]{0:T(128)S(1)}, f32[128]{0:T(128)}, u32[]{:S(2)}) copy-start(f32[128]{0:T(128)} %copy-done.20) | copy-start | bytes 1540
  259.6 24.1 %all-to-all-start.7 = ((bf16[128,8,96]{0,2,1:T(8,128)(2,1)}), bf16[128,8,96]{0,2,1:T(8,128)(2,1)}, u32[]{:S(2)}, u32[]{:S(2)}) async-start(bf16[128,8,96]{0,2,1:T(8,128)(2,1)} %bitcast.107), calls=%async_computation.9 | async-start | bytes 393216 | tf_op jit(solution)/shard_map/all_to_all | solution.py:78
  263.8 79.9 %reduce-scatter.5.cloned.1.call-start = ((), (), s32[]{:S(2)}) async-start(), calls=%async_computation.17 | async-start | bytes 1769472 | tf_op jit(solution)/shard_map/reduce_scatter | solution.py:211
  265.8 4.6 %copy-start.3 = (f32[128,768]{1,0:T(8,128)S(1)}, f32[128,768]{1,0:T(8,128)}, u32[]{:S(2)}) copy-start(f32[128,768]{1,0:T(8,128)} %copy-done.2) | copy-start | bytes 1179652
  265.8 4.6 %copy-start.12 = (bf16[128,768]{1,0:T(8,128)(2,1)S(1)}, bf16[128,768]{1,0:T(8,128)(2,1)}, u32[]{:S(2)}) copy-start(bf16[128,768]{1,0:T(8,128)(2,1)} %param.29) | copy-start | bytes 589828
  283.7 10.9 %all-to-all-start.5 = ((f32[8,1,768]{2,1,0:T(1,128)}), f32[8,1,768]{2,1,0:T(1,128)S(1)}, u32[]{:S(2)}, u32[]{:S(2)}) async-start(f32[8,1,768]{2,1,0:T(1,128)} %all_to_all.113), calls=%async_computation.7 | async-start | bytes 49152 | tf_op jit(solution)/shard_map/all_to_all | solution.py:78
  290.7 8.1 %copy-start.29 = (f32[384]{0:T(512)S(1)}, f32[384]{0:T(512)}, u32[]{:S(2)}) copy-start(f32[384]{0:T(512)} %get-tuple-element.51) | copy-start | bytes 4612
  294.6 13.4 %all-to-all-start.8 = ((bf16[4,96,768]{2,1,0:T(8,128)(2,1)}), bf16[4,96,768]{2,1,0:T(8,128)(2,1)}, u32[]{:S(2)}, u32[]{:S(2)}) async-start(bf16[4,96,768]{2,1,0:T(8,128)(2,1)} %pad_maximum_fusion.2), calls=%async_computation.10 | async-start | bytes 1179648 | tf_op jit(solution)/shard_map/all_to_all | solution.py:78
  308.7 7.9 %all-to-all-start.6 = ((f32[4,1,1152]{2,1,0:T(1,128)}), f32[4,1,1152]{2,1,0:T(1,128)S(1)}, u32[]{:S(2)}, u32[]{:S(2)}) async-start(f32[4,1,1152]{2,1,0:T(1,128)} %broadcast_in_dim.37), calls=%async_computation.8 | async-start | bytes 36864 | tf_op jit(solution)/shard_map/all_to_all | solution.py:78
  316.6 11.0 %all-to-all-start.9 = ((bf16[8,24,288]{2,1,0:T(8,128)(2,1)}), bf16[8,24,288]{2,1,0:T(8,128)(2,1)}, u32[]{:S(2)}, u32[]{:S(2)}) async-start(bf16[8,24,288]{2,1,0:T(8,128)(2,1)} %all_to_all.109), calls=%async_computation.11 | async-start | bytes 294912 | tf_op jit(solution)/shard_map/all_to_all | solution.py:78
  329.7 12.0 %all-to-all-start.10 = ((bf16[4,96,768]{2,1,0:T(8,128)(2,1)}), bf16[4,96,768]{2,1,0:T(8,128)(2,1)S(1)}, u32[]{:S(2)}, u32[]{:S(2)}) async-start(bf16[4,96,768]{2,1,0:T(8,128)(2,1)} %broadcast_in_dim.68), calls=%async_computation.12 | async-start | bytes 1179648 | tf_op jit(solution)/shard_map/all_to_all | solution.py:78
  (14 other events, 31.9 us)
Sparse Core Ops, SparseCore 0:
  9.7 49.0 all-gather.6
  90.9 23.5 all-gather.8
  116.1 33.6 all-gather.10
  162.0 33.8 reduce-scatter.2
  197.3 25.0 all-gather.14
  224.5 29.5 all-gather.12
  266.9 35.7 reduce-scatter.4
